TPU v7x, 1024 devices: a whole 8x8x8 slice. The times are simulated.
1024 devices in a mesh: pipe: 8 (over z), dp: 32 (over x, y_hi), tensor: 4 (over y_lo, core).
Axes of the slice: x: 8, y: 8 (y_hi: 4, y_lo: 2; y = y_hi * 2 + y_lo), z: 8, core: 2. Of those that a mesh axis runs over, the one named last changes fastest.
Arguments:
- queries: bfloat16 [8, 4096, 8192], P('pipe', 'dp', 'tensor'), may hold values from -5.5 to 5.5
- cache_keys: bfloat16 [4096, 4, 8, 256], P('dp', 'tensor', 'pipe'), may hold values from -5.5 to 5.5
- cache_values: bfloat16 [4096, 4, 8, 256], P('dp', 'tensor', 'pipe'), may hold values from -40 to 40
- doc_lengths: int32 [32, 6], P('dp'), may hold values from 1 to 64, 128 in all within a row
- row_counts: int32 [32, 32], replicated, may hold values from 3 to 5, as said below
- out_gain: bfloat16 [8192], P('tensor'), may hold values from 0.099609375 to 1.8984375
Outputs:
- regrouped: bfloat16 [8, 4096, 8192], P('pipe', 'dp', 'tensor')
Inputs may be any that keep to these rules, and one draw needn't show every extreme that they name: row_counts[i, j] is how many rows data group i sends to data group j; each row and each column of row_counts sums to 128; some entry equals 5 in every draw.
All inputs are finite; a program needn't handle non-finite values.
Results may differ from a plain program's by a relative error of at most 0.0085.
Values may be sent and summed in bfloat16 or wider, within the bound.
A program may use at most 32 MiB of HBM per device.

v0:
```python
import jax
import jax.numpy as jnp
from jax import lax
from jax.sharding import PartitionSpec as P

HEADS = 64
HEAD_DIM = 128


masked_fill = -1e30
norm_eps = 1e-06


def doc_ids(ends, positions):
    return jnp.sum((positions[:, None] >= ends[None, :]).astype(jnp.int32), axis=1)


def body(queries, cache_keys, cache_values, doc_lengths, row_counts, out_gain):
    query = queries[0]
    seq = query.shape[0]
    local_width = query.shape[1]
    heads_dev = local_width // HEAD_DIM
    width = HEADS * HEAD_DIM
    scale = 1.0 / HEAD_DIM**0.5
    ends = jnp.cumsum(doc_lengths[0])
    positions = jnp.arange(seq, dtype=jnp.int32)
    docs = doc_ids(ends, positions)
    allowed = (docs[:, None] == docs[None, :]) & (positions[None, :] <= positions[:, None])
    all_keys, all_values = (
        lax.all_gather(cache_keys, "pipe", axis=2, tiled=True),
        lax.all_gather(cache_values, "pipe", axis=2, tiled=True),
    )
    query_heads = query.reshape(seq, heads_dev, HEAD_DIM)
    scores = (
        jnp.einsum(
            "qhd,khd->hqk",
            query_heads,
            all_keys.reshape(seq, heads_dev, HEAD_DIM),
            preferred_element_type=jnp.float32,
        )
        * scale
    )
    scores = jnp.where(allowed[None], scores, masked_fill)
    top = jnp.max(scores, axis=2)
    weights = jnp.where(allowed[None], jnp.exp(scores - top[:, :, None]), 0.0)
    total = jnp.sum(weights, axis=2)
    accum = jnp.einsum(
        "hqk,khd->hqd",
        weights.astype(jnp.bfloat16),
        all_values.reshape(seq, heads_dev, HEAD_DIM),
        preferred_element_type=jnp.float32,
    )
    count = query_heads.shape[1]
    attn = (
        (accum / total[:, :, None])
        .transpose(1, 0, 2)
        .reshape(seq, count * HEAD_DIM)
        .astype(jnp.bfloat16)
    )
    wide = attn.astype(jnp.float32)
    squares = jnp.sum(wide * wide, axis=1)
    gain = out_gain.astype(jnp.float32)
    groups = lax.axis_size("dp")
    own_group = lax.axis_index("dp")
    capacity = 5 * seq // (4 * groups)
    outgoing = lax.dynamic_index_in_dim(row_counts, own_group, 0, keepdims=False)
    incoming = lax.dynamic_index_in_dim(row_counts, own_group, 1, keepdims=False)
    send_start = jnp.cumsum(outgoing) - outgoing
    slot_ids = jnp.arange(capacity, dtype=jnp.int32)
    valid = (slot_ids[None, :] < outgoing[:, None]).reshape(-1)
    send_rows = jnp.where(valid, (send_start[:, None] + slot_ids[None, :]).reshape(-1), 0)
    col_end = jnp.cumsum(incoming)
    source = jnp.sum((positions[:, None] >= col_end[None, :]).astype(jnp.int32), axis=1)
    onehot = (source[:, None] == jnp.arange(groups, dtype=jnp.int32)[None, :]).astype(jnp.int32)
    begin_of = jnp.sum(onehot * (col_end - incoming)[None, :], axis=1)
    recv_rows = source * capacity + positions - begin_of
    row_total = lax.psum(squares, "tensor")
    normed = (wide * lax.rsqrt(row_total / width + norm_eps)[:, None] * gain[None, :]).astype(
        jnp.bfloat16
    )
    picked = jnp.take(normed, send_rows, axis=0)
    keep = valid.reshape((valid.shape[0],) + (1,) * (normed.ndim - 1))
    picked = jnp.where(keep, picked, jnp.zeros_like(picked))
    got_rows = lax.all_to_all(
        picked.reshape((groups, capacity) + normed.shape[1:]),
        "dp",
        split_axis=0,
        concat_axis=0,
        tiled=True,
    )
    flat = got_rows.reshape((groups * capacity,) + got_rows.shape[2:])
    result = jnp.take(flat, recv_rows, axis=0)
    return result[None]


def solution(mesh):
    return jax.shard_map(
        body,
        mesh=mesh,
        in_specs=(
            P("pipe", "dp", "tensor"),
            P("dp", "tensor", "pipe", None),
            P("dp", "tensor", "pipe", None),
            P("dp", None),
            P(),
            P("tensor"),
        ),
        out_specs=P("pipe", "dp", "tensor"),
        check_vma=False,
    )
```

profile of v0, /device:TPU:1, one launch (start us, length us, event | category | flops | bytes accessed | tf_op | source)
XLA Modules:
  0.0 121.9 jit_solution(17009093749700639309)
XLA Ops:
  0.0 0.7 fusion.13
  0.7 0.1 copy.28
  0.9 0.1 reduce.3
  1.0 0.6 copy-done.3
  1.8 32.7 %all_gather.6 = bf16[128,1,8,256]{3,0,1,2:T(8,128)(2,1)S(1)} all-gather(bf16[128,1,1,256]{3,0,1,2:T(8,128)(2,1)S(1)} %bitcast.46), channel_id=1, replica_groups=mesh['pipe'=8,'dp'=32,'tensor'=4] {'pipe'}, dimensions={2}, use_global_device_ids=true | all-gather | bytes 589824 | tf_op jit(solution)/shard_map/all_gather | solution.py:30
  34.5 0.3 copy.30
  34.8 0.8 copy-done
  35.5 0.1 copy.39
  35.6 0.6 copy-done.5
  36.3 0.2 reduce-window.25
  36.7 0.5 fusion.5
  37.2 0.3 fusion.19
  37.4 0.6 copy-done.2
  38.0 19.3 %all_gather.7 = bf16[128,1,8,256]{3,0,1,2:T(8,128)(2,1)S(1)} all-gather(bf16[128,1,1,256]{3,0,1,2:T(8,128)(2,1)S(1)} %bitcast.47), channel_id=1, replica_groups=mesh['pipe'=8,'dp'=32,'tensor'=4] {'pipe'}, dimensions={2}, use_global_device_ids=true | all-gather | bytes 589824 | tf_op jit(solution)/shard_map/all_gather | solution.py:31
  57.4 0.3 copy.34
  57.6 0.5 multiply_reduce_fusion
  58.1 0.3 copy.36
  58.5 0.3 copy-done.4
  58.8 18.0 %psum.7 = f32[128]{0:T(128)S(1)} all-reduce(f32[128]{0:T(128)S(1)} %get-tuple-element.11), channel_id=1, replica_groups=mesh['pipe'=8,'dp'=32,'tensor'=4] {'tensor'}, use_global_device_ids=true, to_apply=%region_9.10 | all-reduce | flops 128 | bytes 1024 | tf_op jit(solution)/shard_map/psum | solution.py:77
  76.8 0.1 select_n.90
  76.9 0.2 multiply_convert_fusion
  77.1 1.0 gather_fusion
  78.2 0.3 gather.13
  78.4 1.2 %select_select_fusion = bf16[32,5,2048]{2,1,0:T(8,128)(2,1)} fusion(bf16[32,5,2048]{2,1,0:T(8,128)(2,1)S(1)} %gather.13, pred[32,5]{1,0:T(8,128)(4,1)S(1)} %get-tuple-element.10, pred[32,5]{1,0:T(8,128)(4,1)S(1)} %get-tuple-element.9), kind=kLoop, calls=%fused_computation.12 | loop fusion | flops 655360 | bytes 1311040 | tf_op jit(solution)/shard_map/jit(_where)/select_n | solution.py:83
  79.6 12.3 %all-to-all-start = ((bf16[32,5,2048]{2,1,0:T(8,128)(2,1)}), bf16[32,5,2048]{2,1,0:T(8,128)(2,1)S(1)}, u32[]{:S(2)}, u32[]{:S(2)}) async-start(bf16[32,5,2048]{2,1,0:T(8,128)(2,1)} %select_select_fusion), calls=%async_computation | async-start | bytes 2097152 | tf_op jit(solution)/shard_map/all_to_all | solution.py:84
  91.9 0.2 fusion.16
  92.1 0.1 reduce.1
  92.4 0.1 select_reduce_fusion
  92.5 27.3 %all-to-all-done = bf16[32,5,2048]{2,1,0:T(8,128)(2,1)S(1)} async-done(((bf16[32,5,2048]{2,1,0:T(8,128)(2,1)}), bf16[32,5,2048]{2,1,0:T(8,128)(2,1)S(1)}, u32[]{:S(2)}, u32[]{:S(2)}) %all-to-all-start) | async-done | bytes 655392 | tf_op jit(solution)/shard_map/all_to_all | solution.py:84
  119.7 0.3 reshape.293
  120.0 0.9 gather_fusion.1
  121.0 0.9 bitcast_select_fusion
  (23 shorter events, 0.6 us)
Async XLA Ops:
  0.0 1.8 %copy-start.1 = (bf16[128,1,1,256]{3,0,2,1:T(8,128)(2,1)S(1)}, bf16[128,1,1,256]{3,0,2,1:T(8,128)(2,1)}, u32[]{:S(2)}) copy-start(bf16[128,1,1,256]{3,0,2,1:T(8,128)(2,1)} %param.7) | copy-start | bytes 196612
  0.9 0.7 copy-start.3
  34.5 1.0 copy-start
  35.6 0.7 copy-start.5
  37.2 0.8 copy-start.2
  58.1 0.7 copy-start.4
  79.6 40.1 %all-to-all-start = ((bf16[32,5,2048]{2,1,0:T(8,128)(2,1)}), bf16[32,5,2048]{2,1,0:T(8,128)(2,1)S(1)}, u32[]{:S(2)}, u32[]{:S(2)}) async-start(bf16[32,5,2048]{2,1,0:T(8,128)(2,1)} %select_select_fusion), calls=%async_computation | async-start | bytes 2097152 | tf_op jit(solution)/shard_map/all_to_all | solution.py:84
where the time goes:
time: 124 us; the launch traced here: 122 us
  blocking collectives  70 us (56%)
  waiting for transfers between devices  27.3 us (22%)
  starting transfers between devices  12.3 us (10%)
  local copies, waits for them, and re-layouts  7.54 us (6%)
  other arithmetic  3.63 us (3%)
    all_gather x1, blocking collectives, body(): lax.all_gather(cache_keys, 'pipe', axis=2, tiled=True)  32.7 us
    all_to_all x1, waiting for transfers between devices, body(): lax.all_to_all(picked.reshape((groups, capacity) + normed.shape[1:]), 'dp...  27.3 us
    all_gather x1, blocking collectives, body(): lax.all_gather(cache_values, 'pipe', axis=2, tiled=True)  19.3 us
    psum x1, blocking collectives, body(): row_total = lax.psum(squares, 'tensor')  18 us
    all_to_all x1, starting transfers between devices, body(): lax.all_to_all(picked.reshape((groups, capacity) + normed.shape[1:]), 'dp...  12.3 us
    unnamed x13, local copies, waits for them, and re-layouts  3.06 us
  transfers between devices with their start and end apart: 1, of which 1 were waited for; matrix products, arithmetic and copies ran while one was open for 0% of the time, Pallas kernels for 0%

commit v1 on v0

v1 whole, which is shorter than its diff:
```python
import functools

import jax
import jax.numpy as jnp
from jax import lax
from jax.experimental import pallas as pl
from jax.experimental.pallas import tpu as pltpu
from jax.sharding import PartitionSpec as P

HEADS = 64
HEAD_DIM = 128

masked_fill = -1e30
norm_eps = 1e-06
MESH = pl.DeviceIdType.MESH
BLOCKS_PER_GROUP = 2


def dot(a, b, contract, **options):
    return lax.dot_general(a, b, (contract, ((), ())), preferred_element_type=jnp.float32, **options)


def iota(shape, dim):
    return lax.broadcasted_iota(jnp.int32, shape, dim)


def kernel(
    sizes,
    queries,
    keys,
    values,
    doc_lengths,
    row_counts,
    out_gain,
    out,
    query,
    cache,
    shape_buf,
    outbox,
    inbox,
    rows_buf,
    result,
    sums,
    load_sem,
    key_send,
    key_recv,
    value_send,
    value_recv,
    row_send,
    row_recv,
    sum_send,
    sum_recv,
):
    n_pipe, n_dp, n_tensor, seq, cap, n_docs = sizes
    half = n_pipe // 2
    slots = n_dp * cap
    block_width = cache.shape[-1]
    heads_block = block_width // HEAD_DIM
    heads_group = BLOCKS_PER_GROUP * heads_block
    groups = n_pipe // BLOCKS_PER_GROUP
    y_size = 4 if n_dp >= 4 else n_dp
    x_size = n_dp // y_size
    pipe = lax.axis_index("pipe")
    me = lax.axis_index("dp")
    tensor = lax.axis_index("tensor")
    right = {"pipe": lax.rem(pipe + 1, n_pipe)}
    left = {"pipe": lax.rem(pipe + n_pipe - 1, n_pipe)}

    def length(offset, size):
        return min(offset, size - offset)

    offsets = sorted(
        ((dx, dy) for dx in range(x_size) for dy in range(y_size) if dx or dy),
        key=lambda o: -length(o[0], x_size) - 2 * length(o[1], y_size),
    )
    x = me // y_size
    y = lax.rem(me, y_size)
    partners = [
        lax.rem(x + dx, x_size) * y_size + lax.rem(y + dy, y_size) for dx, dy in offsets
    ]
    tensor_peers = [lax.rem(tensor + k, n_tensor) for k in range(1, n_tensor)]

    barrier = pltpu.get_barrier_semaphore()
    devices = [right, left]
    devices += [{"tensor": t} for t in tensor_peers]
    devices += [{"dp": j} for j in partners]
    for device in devices:
        pl.semaphore_signal(barrier, inc=1, device_id=device, device_id_type=MESH)
    loads = [
        pltpu.make_async_copy(keys, cache.at[0, 0], load_sem.at[0]),
        pltpu.make_async_copy(values, cache.at[0, 1], load_sem.at[1]),
        pltpu.make_async_copy(queries.at[0], query, load_sem.at[2]),
    ]
    for load in loads:
        load.start()

    row = iota((seq, seq), 0)
    col = iota((seq, seq), 1)
    end = jnp.int32(0)
    row_doc = jnp.zeros((seq, seq), jnp.int32)
    col_doc = jnp.zeros((seq, seq), jnp.int32)
    for k in range(n_docs):
        end = end + doc_lengths[0, k]
        row_doc = row_doc + (row >= end).astype(jnp.int32)
        col_doc = col_doc + (col >= end).astype(jnp.int32)
    allowed = (row_doc == col_doc) & (col <= row)

    counts = row_counts[...].astype(jnp.float32)
    group_row = iota((n_dp, n_dp), 0)
    group_col = iota((n_dp, n_dp), 1)
    own_counts = jnp.sum(jnp.where(group_row == me, counts, 0.0), axis=0, keepdims=True)
    slot_of = iota((slots, n_dp), 0)
    lane_of = iota((slots, n_dp), 1)
    starts_at = lane_of * cap
    before = (starts_at + cap <= slot_of).astype(jnp.float32)
    same = ((starts_at <= slot_of) & (slot_of < starts_at + cap)).astype(jnp.float32)
    slot_col = iota((slots, 1), 0).astype(jnp.float32)
    index = slot_col - cap * jnp.sum(before, axis=1, keepdims=True)
    token = iota((slots, seq), 1).astype(jnp.float32)

    send_count = jnp.sum(same * own_counts, axis=1, keepdims=True)
    send_start = jnp.sum(before * own_counts, axis=1, keepdims=True)
    pick = (token == send_start + index) & (index < send_count)
    pick = pick.astype(jnp.float32).astype(jnp.bfloat16)

    narrow = counts.astype(jnp.bfloat16)
    mine = lane_of == me
    contract = ((1,), (0,))
    recv_count = dot(same.astype(jnp.bfloat16), narrow, contract)
    recv_count = jnp.sum(jnp.where(mine, recv_count, 0.0), axis=1, keepdims=True)
    recv_start = dot(before.astype(jnp.bfloat16), narrow, contract)
    recv_start = jnp.sum(jnp.where(mine, recv_start, 0.0), axis=1, keepdims=True)
    place = (token == recv_start + index) & (index < recv_count)
    place = jnp.transpose(place.astype(jnp.float32)).astype(jnp.bfloat16)

    for load in loads[:2]:
        load.wait()
    pl.semaphore_wait(barrier, len(devices))

    def ring(slot, into, part, way, step):
        send, recv = (key_send, key_recv) if part == 0 else (value_send, value_recv)
        return pltpu.make_async_remote_copy(
            src_ref=cache.at[slot, part],
            dst_ref=cache.at[into, part],
            send_sem=send.at[way, step],
            recv_sem=recv.at[way, step],
            device_id=left if way else right,
            device_id_type=MESH,
        )

    hops = {}

    def forward(step):
        for part in (0, 1):
            for way in (0, 1):
                if step + 1 == half and part != way:
                    continue
                slot = 0 if step == 0 else 2 * step - 1 + way
                into = 2 * half - 1 if step + 1 == half else 2 * step + 1 + way
                hops[part, way, step] = ring(slot, into, part, way, step)
                hops[part, way, step].start()

    def arrive(step):
        for part in (0, 1):
            for way in (0, 1):
                if (part, way, step - 1) in hops:
                    hops[part, way, step - 1].wait_recv()

    def source(block):
        if block == 0:
            return pipe
        d = (block + 1) // 2
        return lax.rem(pipe + (d if block % 2 == 0 else n_pipe - d), n_pipe)

    scale = 1.0 / HEAD_DIM**0.5

    def attend(block):
        for h in range(heads_block):
            lanes = pl.ds(h * HEAD_DIM, HEAD_DIM)
            column = pl.multiple_of(source(block) * block_width + h * HEAD_DIM, HEAD_DIM)
            scores = dot(query[:, pl.ds(column, HEAD_DIM)], cache[block, 0, :, lanes], ((1,), (1,)))
            scores = jnp.where(allowed, scores * scale, masked_fill)
            top = jnp.max(scores, axis=1, keepdims=True)
            weights = jnp.where(allowed, jnp.exp(scores - top), 0.0)
            total = jnp.sum(weights, axis=1, keepdims=True)
            accum = dot(weights.astype(jnp.bfloat16), cache[block, 1, :, lanes], ((1,), (0,)))
            attn = (accum / total).astype(jnp.bfloat16)
            picked = dot(pick, attn, ((1,), (0,)))
            shape_buf[:, (block % BLOCKS_PER_GROUP) * heads_block + h, :] = picked

    def send_rows(group):
        outbox[group] = shape_buf[...].astype(jnp.bfloat16)
        mine = pl.ds(me * cap, cap)
        for j in partners:
            pltpu.make_async_remote_copy(
                src_ref=outbox.at[group, pl.ds(j * cap, cap)],
                dst_ref=inbox.at[group, mine],
                send_sem=row_send.at[group],
                recv_sem=row_recv.at[group],
                device_id={"dp": j},
                device_id_type=MESH,
            ).start()
        inbox[group, mine] = outbox[group, mine]

    def whole(group, sem):
        most = pl.ds(0, slots - cap)
        return pltpu.make_async_copy(outbox.at[group, most], inbox.at[group, most], sem.at[group])

    forward(0)
    loads[2].wait()
    arrived = 0
    for block in range(n_pipe):
        need = (block + 1) // 2
        if need > arrived:
            arrive(need)
            arrived = need
            if need < half:
                forward(need)
        attend(block)
        if (block + 1) % BLOCKS_PER_GROUP == 0:
            send_rows(block // BLOCKS_PER_GROUP)

    squares = jnp.zeros((seq, HEAD_DIM), jnp.float32)
    for group in range(groups):
        whole(group, row_recv).wait()
        rows_buf[...] = inbox[group].astype(jnp.float32)
        for h in range(heads_group):
            rows = dot(place, rows_buf[:, h, :].astype(jnp.bfloat16), ((1,), (0,)))
            result[group * heads_group + h] = rows
            squares = squares + rows * rows
    ones = jnp.ones((8, HEAD_DIM), jnp.float32)
    sums[0] = dot(ones, squares, ((1,), (1,)), precision=lax.Precision.HIGHEST)
    copies = []
    for k, t in enumerate(tensor_peers):
        copies.append(
            pltpu.make_async_remote_copy(
                src_ref=sums.at[0],
                dst_ref=sums.at[1 + k],
                send_sem=sum_send.at[k],
                recv_sem=sum_recv.at[k],
                device_id={"tensor": t},
                device_id_type=MESH,
            )
        )
        copies[-1].start()
    for copy in copies:
        copy.wait_recv()
    total = sums[0]
    for k in range(1, n_tensor):
        total = total + sums[k]
    total = jnp.broadcast_to(total[0:1], (seq, seq))
    factor = lax.rsqrt(jnp.transpose(total) / (HEADS * HEAD_DIM) + norm_eps)
    for block in range(n_pipe):
        for h in range(heads_block):
            lanes = pl.ds(pl.multiple_of(source(block) * block_width + h * HEAD_DIM, HEAD_DIM), HEAD_DIM)
            gain = out_gain[:, lanes].astype(jnp.float32)
            out[0, :, lanes] = (result[block * heads_block + h] * factor * gain).astype(jnp.bfloat16)

    for hop in hops.values():
        hop.wait_send()
    for group in range(groups):
        whole(group, row_send).wait()
    for copy in copies:
        copy.wait_send()


def body(queries, cache_keys, cache_values, doc_lengths, row_counts, out_gain):
    n_pipe, n_dp, n_tensor = (lax.axis_size(name) for name in ("pipe", "dp", "tensor"))
    seq, width = queries.shape[1:]
    block_width = cache_keys.shape[-1]
    cap = 5 * seq // (4 * n_dp)
    slots = n_dp * cap
    heads_group = BLOCKS_PER_GROUP * block_width // HEAD_DIM
    groups = n_pipe // BLOCKS_PER_GROUP
    half = n_pipe // 2
    sizes = (n_pipe, n_dp, n_tensor, seq, cap, doc_lengths.shape[1])
    vmem = pl.BlockSpec(memory_space=pltpu.VMEM)
    smem = pl.BlockSpec(memory_space=pltpu.SMEM)
    anywhere = pl.BlockSpec(memory_space=pl.ANY)
    dma = pltpu.SemaphoreType.DMA
    return pl.pallas_call(
        functools.partial(kernel, sizes),
        out_shape=jax.ShapeDtypeStruct(queries.shape, queries.dtype),
        in_specs=[anywhere, anywhere, anywhere, smem, vmem, vmem],
        out_specs=vmem,
        scratch_shapes=[
            pltpu.VMEM((seq, width), jnp.bfloat16),
            pltpu.VMEM((n_pipe, 2, seq, block_width), jnp.bfloat16),
            pltpu.VMEM((slots, heads_group, HEAD_DIM), jnp.float32),
            pltpu.VMEM((groups, slots, heads_group, HEAD_DIM), jnp.bfloat16),
            pltpu.VMEM((groups, slots, heads_group, HEAD_DIM), jnp.bfloat16),
            pltpu.VMEM((slots, heads_group, HEAD_DIM), jnp.float32),
            pltpu.VMEM((width // HEAD_DIM, seq, HEAD_DIM), jnp.float32),
            pltpu.VMEM((n_tensor, 8, HEAD_DIM), jnp.float32),
            dma((3,)),
            dma((2, half)),
            dma((2, half)),
            dma((2, half)),
            dma((2, half)),
            dma((groups,)),
            dma((groups,)),
            dma((n_tensor - 1,)),
            dma((n_tensor - 1,)),
        ],
        compiler_params=pltpu.CompilerParams(collective_id=0, has_side_effects=True),
        name="attend_regroup",
    )(
        queries,
        cache_keys.reshape(seq, block_width),
        cache_values.reshape(seq, block_width),
        doc_lengths,
        row_counts,
        out_gain.reshape(1, width),
    )


def solution(mesh):
    return jax.shard_map(
        body,
        mesh=mesh,
        in_specs=(
            P("pipe", "dp", "tensor"),
            P("dp", "tensor", "pipe", None),
            P("dp", "tensor", "pipe", None),
            P("dp", None),
            P(),
            P("tensor"),
        ),
        out_specs=P("pipe", "dp", "tensor"),
        check_vma=False,
    )
```

time: 124 us -> 59.7 us (0.48); the launches traced: 122 us -> 59.4 us
  blocking collectives: 70 us -> 0 us
  Pallas kernels: 0 us -> 56.2 us
  waiting for transfers between devices: 27.3 us -> 0 us
  starting transfers between devices: 12.3 us -> 0 us
  local copies, waits for them, and re-layouts: 7.54 us -> 3.17 us
  other arithmetic: 3.63 us -> 0 us
    pallas_call x0 -> x1, Pallas kernels: none -> 56.2 us  [body(): pl.pallas_call(functools.partial(kernel, sizes), out_shape=jax.ShapeDtype...]
    all_gather x2 -> x0, blocking collectives: 52 us -> none  [the longest x1 32.7 us: body(): lax.all_gather(cache_keys, 'pipe', axis=2, tiled=True)]
    all_to_all x1 -> x0, waiting for transfers between devices: 27.3 us -> none  [body(): lax.all_to_all(picked.reshape((groups, capacity) + normed.shape[1:]), 'dp...]
    psum x1 -> x0, blocking collectives: 18 us -> none  [body(): row_total = lax.psum(squares, 'tensor')]
    all_to_all x1 -> x0, starting transfers between devices: 12.3 us -> none  [body(): lax.all_to_all(picked.reshape((groups, capacity) + normed.shape[1:]), 'dp...]
    gather x3 -> x0, local copies, waits for them, and re-layouts: 2.23 us -> none  [the longest x2 1.3 us: body(): picked = jnp.take(normed, send_rows, axis=0)]
    select_n x5 -> x0, other arithmetic: 2.22 us -> none  [the longest x1 1.22 us: body(): picked = jnp.where(keep, picked, jnp.zeros_like(picked))]
    unnamed x13 -> x1, local copies, waits for them, and re-layouts: 3.06 us -> 1.88 us
  transfers between devices with their start and end apart: 1 -> 0, of which waited for: 1 -> 0; matrix products, arithmetic and copies ran while one was open for 0% -> 0% of each run, Pallas kernels for 0% -> 0%
where the time goes in v1:
time: 59.7 us; the launch traced here: 59.4 us
  Pallas kernels  56.2 us (94%)
  local copies, waits for them, and re-layouts  3.17 us (5%)
    pallas_call x1, Pallas kernels, body(): pl.pallas_call(functools.partial(kernel, sizes), out_shape=jax.ShapeDtype...  56.2 us
    unnamed x1, local copies, waits for them, and re-layouts  1.88 us
    reshape x1, local copies, waits for them, and re-layouts, body(): out_gain.reshape(1, width)  1.29 us

profile of v1, /device:TPU:1, one launch (start us, length us, event | category | flops | bytes accessed | tf_op | source)
XLA Modules:
  0.0 59.4 jit_solution(1645216817973731961)
XLA Ops:
  0.0 1.3 %reshape.11.out_gain = bf16[1,2048]{1,0:T(2,128)(2,1)} reshape(bf16[2048]{0:T(1024)(128)(2,1)} %param.11) | data formatting | bytes 8192 | tf_op jit(solution)/shard_map/reshape | solution.py:313
  1.3 56.2 %attend_regroup.1 = bf16[1,128,2048]{2,1,0:T(8,128)(2,1)} custom-call(bf16[1,128,2048]{2,1,0:T(8,128)(2,1)} %queries.1, bf16[128,256]{1,0:T(8,128)(2,1)} %bitcast.2, bf16[128,256]{1,0:T(8,128)(2,1)} %bitcast.3, s32[1,6]{1,0:T(1,128)} %doc_lengths.1, s32[32,32]{1,0:T(8,128)} %row_counts.1, bf16[1,2048]{1,0:T(2,128)(2,1)} %reshape.11.out_gain), custom_call_target="tpu_custom_call" | custom-call | tf_op jit(solution)/shard_map/attend_regroup/pallas_call | solution.py:281
  57.5 1.9 %copy.8 = bf16[1,128,2048]{2,1,0:T(8,128)(2,1)} copy(bf16[1,128,2048]{2,1,0:T(8,128)(2,1)} %attend_regroup.1) | data formatting | bytes 1048576

commit v2 on v1

v2 whole, which is shorter than its diff:
```python
import functools

import jax
import jax.numpy as jnp
from jax import lax
from jax.experimental import pallas as pl
from jax.experimental.pallas import tpu as pltpu
from jax.sharding import PartitionSpec as P

HEADS = 64
HEAD_DIM = 128

masked_fill = -1e30
norm_eps = 1e-06
MESH = pl.DeviceIdType.MESH
HEADS_PER_GROUP = 4


def dot(a, b, contract, **options):
    return lax.dot_general(a, b, (contract, ((), ())), preferred_element_type=jnp.float32, **options)


def iota(shape, dim):
    return lax.broadcasted_iota(jnp.int32, shape, dim)


def kernel(
    sizes,
    queries,
    keys,
    values,
    doc_lengths,
    row_counts,
    out,
    factor_out,
    query,
    cache,
    shape_buf,
    outbox,
    inbox,
    rows_buf,
    result,
    sums,
    load_sem,
    store_sem,
    hop_send,
    hop_recv,
    row_send,
    row_recv,
    sum_send,
    sum_recv,
):
    n_pipe, n_dp, n_tensor, seq, cap, n_docs = sizes
    half = n_pipe // 2
    slots = n_dp * cap
    heads_block = cache.shape[1]
    groups = n_pipe * heads_block // HEADS_PER_GROUP
    y_size = 4 if n_dp >= 4 else n_dp
    x_size = n_dp // y_size
    pipe = lax.axis_index("pipe")
    me = lax.axis_index("dp")
    tensor = lax.axis_index("tensor")
    right = {"pipe": lax.rem(pipe + 1, n_pipe)}
    left = {"pipe": lax.rem(pipe + n_pipe - 1, n_pipe)}

    def length(offset, size):
        return min(offset, size - offset)

    offsets = sorted(
        ((dx, dy) for dx in range(x_size) for dy in range(y_size) if dx or dy),
        key=lambda o: -length(o[0], x_size) - 2 * length(o[1], y_size),
    )
    x = me // y_size
    y = lax.rem(me, y_size)
    partners = [
        lax.rem(x + dx, x_size) * y_size + lax.rem(y + dy, y_size) for dx, dy in offsets
    ]
    tensor_peers = [lax.rem(tensor + k, n_tensor) for k in range(1, n_tensor)]

    barrier = pltpu.get_barrier_semaphore()
    devices = [right, left]
    devices += [{"tensor": t} for t in tensor_peers]
    devices += [{"dp": j} for j in partners]
    for device in devices:
        pl.semaphore_signal(barrier, inc=1, device_id=device, device_id_type=MESH)
    loads = [
        pltpu.make_async_copy(
            array.at[:, pl.ds(h * HEAD_DIM, HEAD_DIM)], cache.at[0, h, part], load_sem.at[h, part]
        )
        for h in range(heads_block)
        for part, array in enumerate((keys, values))
    ]
    loads.append(pltpu.make_async_copy(queries.at[0], query, load_sem.at[heads_block, 0]))
    for load in loads:
        load.start()

    for load in loads[:-1]:
        load.wait()
    pl.semaphore_wait(barrier, len(devices))

    hops = {}

    def order(way):
        return range(heads_block) if way == 0 else range(heads_block - 1, -1, -1)

    def forward(step, way, h, part):
        last = step + 1 == half
        slot = 0 if step == 0 else 2 * step - 1 + way
        into = 2 * half - 1 if last else 2 * step + 1 + way
        copy = pltpu.make_async_remote_copy(
            src_ref=cache.at[slot, h, part],
            dst_ref=cache.at[into, h, part],
            send_sem=hop_send.at[step, way, h, part],
            recv_sem=hop_recv.at[step, way, h, part],
            device_id=left if way else right,
            device_id_type=MESH,
        )
        copy.start()
        hops[step + 1, way, h, part] = copy

    for i in range(heads_block):
        for part in (0, 1):
            for way in (0, 1):
                forward(0, way, order(way)[i], part)

    row = iota((seq, seq), 0)
    col = iota((seq, seq), 1)
    end = jnp.int32(0)
    row_doc = jnp.zeros((seq, seq), jnp.int32)
    col_doc = jnp.zeros((seq, seq), jnp.int32)
    for k in range(n_docs):
        end = end + doc_lengths[0, k]
        row_doc = row_doc + (row >= end).astype(jnp.int32)
        col_doc = col_doc + (col >= end).astype(jnp.int32)
    allowed = (row_doc == col_doc) & (col <= row)

    counts = row_counts[...].astype(jnp.float32)
    group_row = iota((n_dp, n_dp), 0)
    group_col = iota((n_dp, n_dp), 1)
    own_counts = jnp.sum(jnp.where(group_row == me, counts, 0.0), axis=0, keepdims=True)
    slot_of = iota((slots, n_dp), 0)
    lane_of = iota((slots, n_dp), 1)
    starts_at = lane_of * cap
    before = (starts_at + cap <= slot_of).astype(jnp.float32)
    same = ((starts_at <= slot_of) & (slot_of < starts_at + cap)).astype(jnp.float32)
    slot_col = iota((slots, 1), 0).astype(jnp.float32)
    index = slot_col - cap * jnp.sum(before, axis=1, keepdims=True)
    token = iota((slots, seq), 1).astype(jnp.float32)

    send_count = jnp.sum(same * own_counts, axis=1, keepdims=True)
    send_start = jnp.sum(before * own_counts, axis=1, keepdims=True)
    pick = (token == send_start + index) & (index < send_count)
    pick = pick.astype(jnp.float32).astype(jnp.bfloat16)

    narrow = counts.astype(jnp.bfloat16)
    mine = lane_of == me
    contract = ((1,), (0,))
    recv_count = dot(same.astype(jnp.bfloat16), narrow, contract)
    recv_count = jnp.sum(jnp.where(mine, recv_count, 0.0), axis=1, keepdims=True)
    recv_start = dot(before.astype(jnp.bfloat16), narrow, contract)
    recv_start = jnp.sum(jnp.where(mine, recv_start, 0.0), axis=1, keepdims=True)
    place = (token == recv_start + index) & (index < recv_count)
    place = jnp.transpose(place.astype(jnp.float32)).astype(jnp.bfloat16)

    def column(block, h):
        d = (block + 1) // 2
        z = lax.rem(pipe + (d if block % 2 == 0 else n_pipe - d), n_pipe)
        return pl.ds(pl.multiple_of((z * heads_block + h) * HEAD_DIM, HEAD_DIM), HEAD_DIM)

    scale = 1.0 / HEAD_DIM**0.5
    done = []

    def attend(block, h):
        scores = dot(query[:, column(block, h)], cache[block, h, 0], ((1,), (1,)))
        scores = jnp.where(allowed, scores * scale, masked_fill)
        top = jnp.max(scores, axis=1, keepdims=True)
        weights = jnp.where(allowed, jnp.exp(scores - top), 0.0)
        total = jnp.sum(weights, axis=1, keepdims=True)
        accum = dot(weights.astype(jnp.bfloat16), cache[block, h, 1], contract)
        attn = (accum / total).astype(jnp.bfloat16)
        shape_buf[:, len(done) % HEADS_PER_GROUP, :] = dot(pick, attn, contract)
        done.append((block, h))
        if len(done) % HEADS_PER_GROUP == 0:
            send_rows(len(done) // HEADS_PER_GROUP - 1)

    def send_rows(group):
        outbox[group] = shape_buf[...].astype(jnp.bfloat16)
        mine = pl.ds(me * cap, cap)
        for j in partners:
            pltpu.make_async_remote_copy(
                src_ref=outbox.at[group, pl.ds(j * cap, cap)],
                dst_ref=inbox.at[group, mine],
                send_sem=row_send.at[group],
                recv_sem=row_recv.at[group],
                device_id={"dp": j},
                device_id_type=MESH,
            ).start()
        inbox[group, mine] = outbox[group, mine]

    def whole(group, sem):
        most = pl.ds(0, slots - cap)
        return pltpu.make_async_copy(outbox.at[group, most], inbox.at[group, most], sem.at[group])

    loads[-1].wait()
    for h in range(heads_block):
        attend(0, h)
    for step in range(1, half + 1):
        for i in range(heads_block // 2 if step == half else heads_block):
            for part in (0, 1):
                for way in (0, 1):
                    h = order(way)[i]
                    hops[step, way, h, part].wait_recv()
                    if step + 1 < half or (step + 1 == half and i < heads_block // 2):
                        forward(step, way, h, part)
            for way in (0, 1):
                attend(2 * step - 1 if step == half else 2 * step - 1 + way, order(way)[i])

    squares = jnp.zeros((seq, HEAD_DIM), jnp.float32)
    stores = []
    for group in range(groups):
        whole(group, row_recv).wait()
        rows_buf[...] = inbox[group].astype(jnp.float32)
        for i in range(HEADS_PER_GROUP):
            n = group * HEADS_PER_GROUP + i
            rows = dot(place, rows_buf[:, i, :].astype(jnp.bfloat16), contract)
            squares = squares + rows * rows
            result[n] = rows.astype(jnp.bfloat16)
            stores.append(
                pltpu.make_async_copy(result.at[n], out.at[:, column(*done[n])], store_sem.at[n])
            )
            stores[-1].start()
    ones = jnp.ones((8, HEAD_DIM), jnp.float32)
    sums[0] = dot(ones, squares, ((1,), (1,)), precision=lax.Precision.HIGHEST)
    copies = []
    for k, t in enumerate(tensor_peers):
        copies.append(
            pltpu.make_async_remote_copy(
                src_ref=sums.at[0],
                dst_ref=sums.at[1 + k],
                send_sem=sum_send.at[k],
                recv_sem=sum_recv.at[k],
                device_id={"tensor": t},
                device_id_type=MESH,
            )
        )
        copies[-1].start()
    for hop in hops.values():
        hop.wait_send()
    for group in range(groups):
        whole(group, row_send).wait()
    for store in stores:
        store.wait()
    for copy in copies:
        copy.wait()
    total = sums[0]
    for k in range(1, n_tensor):
        total = total + sums[k]
    total = jnp.transpose(jnp.broadcast_to(total[0:1], (seq, seq)))
    factor_out[...] = lax.rsqrt(total / (HEADS * HEAD_DIM) + norm_eps)


def body(queries, cache_keys, cache_values, doc_lengths, row_counts, out_gain):
    n_pipe, n_dp, n_tensor = (lax.axis_size(name) for name in ("pipe", "dp", "tensor"))
    seq, width = queries.shape[1:]
    block_width = cache_keys.shape[-1]
    heads_block = block_width // HEAD_DIM
    heads = width // HEAD_DIM
    cap = 5 * seq // (4 * n_dp)
    slots = n_dp * cap
    groups = heads // HEADS_PER_GROUP
    half = n_pipe // 2
    sizes = (n_pipe, n_dp, n_tensor, seq, cap, doc_lengths.shape[1])
    vmem = pl.BlockSpec(memory_space=pltpu.VMEM)
    smem = pl.BlockSpec(memory_space=pltpu.SMEM)
    anywhere = pl.BlockSpec(memory_space=pl.ANY)
    dma = pltpu.SemaphoreType.DMA
    rows, factor = pl.pallas_call(
        functools.partial(kernel, sizes),
        out_shape=(
            jax.ShapeDtypeStruct((seq, width), jnp.bfloat16),
            jax.ShapeDtypeStruct((seq, seq), jnp.float32),
        ),
        in_specs=[anywhere, anywhere, anywhere, smem, vmem],
        out_specs=(anywhere, vmem),
        scratch_shapes=[
            pltpu.VMEM((seq, width), jnp.bfloat16),
            pltpu.VMEM((n_pipe, heads_block, 2, seq, HEAD_DIM), jnp.bfloat16),
            pltpu.VMEM((slots, HEADS_PER_GROUP, HEAD_DIM), jnp.float32),
            pltpu.VMEM((groups, slots, HEADS_PER_GROUP, HEAD_DIM), jnp.bfloat16),
            pltpu.VMEM((groups, slots, HEADS_PER_GROUP, HEAD_DIM), jnp.bfloat16),
            pltpu.VMEM((slots, HEADS_PER_GROUP, HEAD_DIM), jnp.float32),
            pltpu.VMEM((heads, seq, HEAD_DIM), jnp.bfloat16),
            pltpu.VMEM((n_tensor, 8, HEAD_DIM), jnp.float32),
            dma((heads_block + 1, 2)),
            dma((heads,)),
            dma((half, 2, heads_block, 2)),
            dma((half, 2, heads_block, 2)),
            dma((groups,)),
            dma((groups,)),
            dma((n_tensor - 1,)),
            dma((n_tensor - 1,)),
        ],
        compiler_params=pltpu.CompilerParams(collective_id=0, has_side_effects=True),
        name="attend_regroup",
    )(
        queries,
        cache_keys.reshape(seq, block_width),
        cache_values.reshape(seq, block_width),
        doc_lengths,
        row_counts,
    )
    normed = rows.astype(jnp.float32) * factor[:, :1] * out_gain.astype(jnp.float32)[None, :]
    return normed.astype(jnp.bfloat16)[None]


def solution(mesh):
    return jax.shard_map(
        body,
        mesh=mesh,
        in_specs=(
            P("pipe", "dp", "tensor"),
            P("dp", "tensor", "pipe", None),
            P("dp", "tensor", "pipe", None),
            P("dp", None),
            P(),
            P("tensor"),
        ),
        out_specs=P("pipe", "dp", "tensor"),
        check_vma=False,
    )
```

time: 59.7 us -> 56.8 us (0.951)
  Pallas kernels: 56.2 us -> 52.8 us
  other arithmetic: 0 us -> 2.72 us
  local copies, waits for them, and re-layouts: 3.17 us -> 0.94 us
    pallas_call x1, Pallas kernels: 56.2 us -> 52.8 us  [body(): pl.pallas_call(functools.partial(kernel, sizes), out_shape=(jax.ShapeDtyp...]
    broadcast_in_dim x0 -> x1, other arithmetic: none -> 2.03 us  [body(): return normed.astype(jnp.bfloat16)[None]]
    unnamed x1 -> x0, local copies, waits for them, and re-layouts: 1.88 us -> none
    reshape x1 -> x0, local copies, waits for them, and re-layouts: 1.29 us -> none  [body(): out_gain.reshape(1, width)]
    slice x0 -> x1, local copies, waits for them, and re-layouts: none -> 0.94 us  [body(): factor[:, :1]]
    convert_element_type x0 -> x1, other arithmetic: none -> 0.69 us  [body(): out_gain.astype(jnp.float32)[None, :]]
where the time goes in v2:
time: 56.8 us; the launch traced here: 56.5 us
  Pallas kernels  52.8 us (93%)
  other arithmetic  2.72 us (5%)
  local copies, waits for them, and re-layouts  0.94 us (2%)
    pallas_call x1, Pallas kernels, body(): pl.pallas_call(functools.partial(kernel, sizes), out_shape=(jax.ShapeDtyp...  52.8 us
    broadcast_in_dim x1, other arithmetic, body(): return normed.astype(jnp.bfloat16)[None]  2.03 us

profile of v2, /device:TPU:1, one launch (start us, length us, event | category | flops | bytes accessed | tf_op | source)
XLA Modules:
  0.0 56.5 jit_solution(17473684056167916690)
XLA Ops:
  0.0 0.7 %convert_element_type.10 = f32[2048]{0:T(1024)S(1)} convert(bf16[2048]{0:T(1024)(128)(2,1)} %param.11) | non-fusion elementwise | flops 2048 | bytes 12288 | tf_op jit(solution)/shard_map/convert_element_type | solution.py:312
  0.7 52.8 %attend_regroup.1 = (bf16[128,2048]{1,0:T(8,128)(2,1)}, f32[128,128]{1,0:T(8,128)}) custom-call(bf16[1,128,2048]{2,1,0:T(8,128)(2,1)} %queries.1, bf16[128,256]{1,0:T(8,128)(2,1)} %bitcast.4, bf16[128,256]{1,0:T(8,128)(2,1)} %bitcast.5, s32[1,6]{1,0:T(1,128)} %doc_lengths.1, s32[32,32]{1,0:T(8,128)} %row_counts.1), custom_call_target="tpu_custom_call" | custom-call | tf_op jit(solution)/shard_map/attend_regroup/pallas_call | solution.py:277
  53.5 0.9 %slice_reduce_fusion = f32[128]{0:T(128)S(1)} fusion(f32[128,128]{1,0:T(8,128)} %get-tuple-element.8), kind=kLoop, calls=%fused_computation.2 | loop fusion | bytes 1024 | tf_op jit(solution)/shard_map/slice | solution.py:312
  54.4 2.0 %fusion = bf16[1,128,2048]{2,1,0:T(8,128)(2,1)} fusion(bf16[128,2048]{1,0:T(8,128)(2,1)} %get-tuple-element.7, f32[2048]{0:T(1024)S(1)} %convert_element_type.10, f32[128]{0:T(128)S(1)} %slice_reduce_fusion), kind=kLoop, calls=%fused_computation.1 | loop fusion | flops 1048576 | bytes 1057280 | tf_op jit(solution)/shard_map/broadcast_in_dim | solution.py:313
